TPU v7x, 256 devices: a whole 4x4x8 slice. The times are simulated.
256 devices in a mesh: rows: 32 (over y, z), mem: 8 (over x, core).
Axes of the slice: x: 4, y: 4, z: 8, core: 2. Of those that a mesh axis runs over, the one named last changes fastest.
Arguments:
- ensemble: float32 [64, 32, 192, 384], P('mem', None, 'rows'), may hold values from 0 to 2
- courant: float32 [3, 32, 192, 384], P(None, None, 'rows'), may hold values from -0.22 to 0.22
- obs_column: int32 [512], P('rows'), may hold values from 0 to 73727, as said below
- obs_value: float32 [32, 512], P(None, 'rows'), may hold values from -6 to 6
- obs_var: float32 [32, 512], P(None, 'rows'), may hold values from 0.5 to 8
Outputs:
- analysis: float32 [64, 32, 192, 384], P('mem', None, 'rows')
Inputs may be any that keep to these rules, and one draw needn't show every extreme that they name: `obs_column`: entry p is x * 384 + y with x from (p // 16) * 6 to (p // 16) * 6 + 5.
All inputs are finite; a program needn't handle non-finite values.
Results may differ from a plain program's by a relative error of at most 0.0003.
Values sent between devices are 32-bit elements; how exact they have to be, the bound alone decides.
No kernel may reach another device: no remote copies, remote signals or barrier semaphores. Data moves between devices by JAX's collectives and lax.ppermute only.
A program may use at most 128 MiB of HBM per device.

v0:
```python
import jax
import jax.numpy as jnp
from jax import lax
from jax.sharding import PartitionSpec as P

STEPS = 3
NS_ITERS = 4
DIFFUSION = 0.05


def padded_2(cells, sides, width):
    for axis, dim in sides:
        count = lax.axis_size(axis)
        ends = count - 1
        head = lax.slice_in_dim(cells, 0, width, axis=dim)
        tail = lax.slice_in_dim(cells, cells.shape[dim] - width, cells.shape[dim], axis=dim)
        cells = jnp.concatenate(
            [
                lax.ppermute(tail, axis, [(i, (i + 1) % count) for i in range(ends)]),
                cells,
                lax.ppermute(head, axis, [((i + 1) % count, i) for i in range(ends)]),
            ],
            axis=dim,
        )
    return cells


def joined_along(parts, dim):
    parts = jnp.moveaxis(parts, 0, dim)
    lengths = parts.shape
    return parts.reshape(*lengths[:dim], lengths[dim] * lengths[dim + 1], *lengths[dim + 2 :])


def from_everyone(shard, axis):
    copies = jnp.broadcast_to(shard, (lax.axis_size(axis), *shard.shape))
    return lax.all_to_all(copies, axis, split_axis=0, concat_axis=0, tiled=True)


def collect(shard, axis, dim):
    return joined_along(from_everyone(shard, axis), dim)


def over_copies(shard, axis):
    everything = from_everyone(shard, axis)
    return jnp.sum(everything, axis=0)


def packed_total(arrays, axis):
    ends = [0]
    for a in arrays:
        ends.append(ends[-1] + a.size)
    so_far = over_copies(jnp.concatenate([a.ravel() for a in arrays]), axis)
    return tuple((so_far[b:e].reshape(a.shape) for a, b, e in zip(arrays, ends, ends[1:])))


def advance(padded, courant):
    center = padded[:, :, 1:-1, :]
    below_x = padded[:, :, :-2, :]
    above_x = padded[:, :, 2:, :]
    padded_y = jnp.pad(center, ((0, 0), (0, 0), (0, 0), (1, 1)))
    below_y = padded_y[:, :, :, :-2]
    above_y = padded_y[:, :, :, 2:]
    padded_z = jnp.pad(center, ((0, 0), (1, 1), (0, 0), (0, 0)))
    below_z = padded_z[:, :-2]
    above_z = padded_z[:, 2:]
    change = jnp.zeros_like(center)
    for component, below, above in (
        (0, below_x, above_x),
        (1, below_y, above_y),
        (2, below_z, above_z),
    ):
        velocity = courant[component][None]
        change = (
            change
            - jnp.maximum(velocity, 0.0) * (center - below)
            - jnp.minimum(velocity, 0.0) * (above - center)
            + DIFFUSION * (above + below - 2.0 * center)
        )
    return center + change


def gram_terms(profiles, obs_value, obs_var):
    members_all = profiles.shape[0]
    center = jnp.mean(profiles, axis=0)
    scaling = 1.0 / jnp.sqrt((members_all - 1.0) * obs_var)
    scaled = ((profiles - center[None]) * scaling[None]).reshape(members_all, -1)
    innovation = ((obs_value - center) / jnp.sqrt(obs_var)).reshape(-1)
    gram_part = jnp.dot(scaled, scaled.T, precision=lax.Precision.HIGHEST)
    pull_part = jnp.dot(scaled, innovation, precision=lax.Precision.HIGHEST)
    return (gram_part, pull_part)


def mixing(gram_sum, pull_sum):
    members_all = gram_sum.shape[0]
    identity_matrix = jnp.eye(members_all, dtype=jnp.float32)
    system = identity_matrix + gram_sum
    frobenius = jnp.sqrt(jnp.sum(system * system))

    def newton(iteration, carry):
        iterate, inverse_root = carry
        factor = 0.5 * (
            3.0 * identity_matrix - jnp.dot(inverse_root, iterate, precision=lax.Precision.HIGHEST)
        )
        return (
            jnp.dot(iterate, factor, precision=lax.Precision.HIGHEST),
            jnp.dot(factor, inverse_root, precision=lax.Precision.HIGHEST),
        )

    iterate, inverse_root = lax.fori_loop(
        0, NS_ITERS, newton, (system / frobenius, identity_matrix)
    )
    root_inverse = inverse_root / jnp.sqrt(frobenius)
    mean_shift = jnp.dot(
        root_inverse,
        jnp.dot(root_inverse, pull_sum, precision=lax.Precision.HIGHEST),
        precision=lax.Precision.HIGHEST,
    ) / jnp.sqrt(members_all - 1.0)
    centering = identity_matrix - 1.0 / members_all
    return 1.0 / members_all + jnp.dot(
        centering, mean_shift[:, None] + root_inverse, precision=lax.Precision.HIGHEST
    )


def per_device(ensemble, courant, obs_column, obs_value, obs_var):
    rows_local = ensemble.shape[2]
    width_y = ensemble.shape[3]
    position = lax.axis_index("rows")
    concentration = ensemble
    for step_index in range(STEPS):
        padded = padded_2(concentration, (("rows", 2),), 1)
        concentration = advance(padded, courant)
    members_dev = concentration.shape[0]
    state_vectors = concentration.reshape(members_dev, concentration.shape[1], rows_local * width_y)
    local_column = obs_column - position * (rows_local * width_y)
    profiles = jnp.take(state_vectors, local_column, axis=2)
    gathered = collect(profiles, "mem", 0)
    gram_part, pull_part = gram_terms(gathered, obs_value, obs_var)
    gram_sum, pull_sum = packed_total((gram_part, pull_part), "rows")
    transform_weights = mixing(gram_sum, pull_sum)
    first_member = lax.axis_index("mem") * members_dev
    own_columns = lax.dynamic_slice_in_dim(transform_weights, first_member, members_dev, 1)
    updated_ensemble = jnp.einsum(
        "jk,jzc->kzc",
        own_columns,
        lax.all_gather(state_vectors, "mem", axis=0, tiled=True),
        precision=lax.Precision.HIGHEST,
    )
    return updated_ensemble.reshape(concentration.shape)


def solution(mesh):
    return jax.shard_map(
        per_device,
        mesh=mesh,
        in_specs=(
            P("mem", None, "rows", None),
            P(None, None, "rows", None),
            P("rows"),
            P(None, "rows"),
            P(None, "rows"),
        ),
        out_specs=P("mem", None, "rows", None),
        check_vma=False,
    )
```

profile of v0, /device:TPU:1, one launch (start us, length us, event | category | flops | bytes accessed | tf_op | source)
XLA Modules:
  0.0 191.4 jit_solution(7177170914299280212)
XLA Ops:
  6.5 1.3 fusion.77
  7.9 4.4 %collective-permute-start = (f32[8,32,1,384]{3,1,2,0:T(8,128)S(1)}, f32[8,32,1,384]{3,1,2,0:T(8,128)S(1)}, u32[]{:S(2)}, u32[]{:S(2)}) collective-permute-start(f32[8,32,1,384]{3,1,2,0:T(8,128)S(1)} %get-tuple-element.60), channel_id=1, source_target_pairs={{0,8},{8,16},{16,24},{24,32},{32,40},{40,48},{48,56},{56,64},{64,7... | collective-permute-start | bytes 1179656 | tf_op jit(solution)/shard_map/ppermute | solution.py:19
  13.6 1.3 maximum_bitcast_fusion.2
  14.9 5.1 %collective-permute-done = f32[8,32,1,384]{3,1,2,0:T(8,128)S(1)} collective-permute-done((f32[8,32,1,384]{3,1,2,0:T(8,128)S(1)}, f32[8,32,1,384]{3,1,2,0:T(8,128)S(1)}, u32[]{:S(2)}, u32[]{:S(2)}) %collective-permute-start) | collective-permute-done | bytes 393248 | tf_op jit(solution)/shard_map/ppermute | solution.py:19
  20.0 4.2 %collective-permute-done.1 = f32[8,32,1,384]{3,1,2,0:T(8,128)S(1)} collective-permute-done((f32[8,32,1,384]{3,1,2,0:T(8,128)S(1)}, f32[8,32,1,384]{3,1,2,0:T(8,128)S(1)}, u32[]{:S(2)}, u32[]{:S(2)}) %collective-permute-start.1) | collective-permute-done | bytes 393248 | tf_op jit(solution)/shard_map/ppermute | solution.py:21
  24.2 3.7 %fusion.48 = f32[8,32,6,384]{3,1,2,0:T(8,128)S(1)} fusion(f32[8,32,6,384]{3,1,2,0:T(8,128)S(1)} %copy-done.1, f32[8,32,1,384]{3,1,2,0:T(8,128)S(1)} %collective-permute-done.1, f32[8,32,1,384]{3,1,2,0:T(8,128)S(1)} %collective-permute-done, f32[32,6,384]{2,0,1:T(8,128)S(1)} %get-tuple-element.65, f32[32,6,384]{2,0,1:T(8,128)S(1)} %get-tuple-element.66, ...), kind=kLoop, calls=%fused_computation.68 | loop fusion | flops 20054016 | bytes 7274496 | tf_op jit(solution)/shard_map/add | solution.py:79
  28.0 3.6 %collective-permute-start.2 = (f32[8,32,1,384]{3,1,2,0:T(8,128)S(1)}, f32[8,32,1,384]{3,1,2,0:T(8,128)S(1)}, u32[]{:S(2)}, u32[]{:S(2)}) collective-permute-start(f32[8,32,1,384]{3,1,2,0:T(8,128)S(1)} %get-tuple-element.58), channel_id=1, source_target_pairs={{0,8},{8,16},{16,24},{24,32},{32,40},{40,48},{48,56},{56,64},{64,7... | collective-permute-start | bytes 1179656 | tf_op jit(solution)/shard_map/ppermute | solution.py:19
  32.9 5.5 %collective-permute-done.2 = f32[8,32,1,384]{3,1,2,0:T(8,128)S(1)} collective-permute-done((f32[8,32,1,384]{3,1,2,0:T(8,128)S(1)}, f32[8,32,1,384]{3,1,2,0:T(8,128)S(1)}, u32[]{:S(2)}, u32[]{:S(2)}) %collective-permute-start.2) | collective-permute-done | bytes 393248 | tf_op jit(solution)/shard_map/ppermute | solution.py:19
  38.4 5.7 %collective-permute-done.3 = f32[8,32,1,384]{3,1,2,0:T(8,128)S(1)} collective-permute-done((f32[8,32,1,384]{3,1,2,0:T(8,128)S(1)}, f32[8,32,1,384]{3,1,2,0:T(8,128)S(1)}, u32[]{:S(2)}, u32[]{:S(2)}) %collective-permute-start.3) | collective-permute-done | bytes 393248 | tf_op jit(solution)/shard_map/ppermute | solution.py:21
  44.1 3.7 %fusion.31 = f32[8,32,6,384]{3,1,2,0:T(8,128)S(1)} fusion(f32[8,32,6,384]{3,1,2,0:T(8,128)S(1)} %fusion.48, f32[8,32,1,384]{3,1,2,0:T(8,128)S(1)} %collective-permute-done.3, f32[8,32,1,384]{3,1,2,0:T(8,128)S(1)} %collective-permute-done.2, f32[32,6,384]{2,0,1:T(8,128)S(1)} %get-tuple-element.65, f32[32,6,384]{2,0,1:T(8,128)S(1)} %get-tuple-element.66, ...), kind=kLoop, calls=%fused_computation.49 | loop fusion | flops 20054016 | bytes 7274496 | tf_op jit(solution)/shard_map/add | solution.py:79
  47.9 4.0 %collective-permute-start.4 = (f32[8,32,1,384]{3,1,2,0:T(8,128)S(1)}, f32[8,32,1,384]{3,1,2,0:T(8,128)S(1)}, u32[]{:S(2)}, u32[]{:S(2)}) collective-permute-start(f32[8,32,1,384]{3,1,2,0:T(8,128)S(1)} %get-tuple-element.56), channel_id=1, source_target_pairs={{0,8},{8,16},{16,24},{24,32},{32,40},{40,48},{48,56},{56,64},{64,7... | collective-permute-start | bytes 1179656 | tf_op jit(solution)/shard_map/ppermute | solution.py:19
  53.2 4.5 %collective-permute-done.4 = f32[8,32,1,384]{3,1,2,0:T(8,128)S(1)} collective-permute-done((f32[8,32,1,384]{3,1,2,0:T(8,128)S(1)}, f32[8,32,1,384]{3,1,2,0:T(8,128)S(1)}, u32[]{:S(2)}, u32[]{:S(2)}) %collective-permute-start.4) | collective-permute-done | bytes 393248 | tf_op jit(solution)/shard_map/ppermute | solution.py:19
  57.7 3.9 %collective-permute-done.5 = f32[8,32,1,384]{3,1,2,0:T(8,128)S(1)} collective-permute-done((f32[8,32,1,384]{3,1,2,0:T(8,128)S(1)}, f32[8,32,1,384]{3,1,2,0:T(8,128)S(1)}, u32[]{:S(2)}, u32[]{:S(2)}) %collective-permute-start.5) | collective-permute-done | bytes 393248 | tf_op jit(solution)/shard_map/ppermute | solution.py:21
  61.5 3.7 %fusion.14 = f32[8,32,6,384]{3,1,2,0:T(8,128)S(1)} fusion(f32[8,32,6,384]{3,1,2,0:T(8,128)S(1)} %fusion.31, f32[8,32,1,384]{3,1,2,0:T(8,128)S(1)} %collective-permute-done.5, f32[8,32,1,384]{3,1,2,0:T(8,128)S(1)} %collective-permute-done.4, f32[32,6,384]{2,0,1:T(8,128)S(1)} %get-tuple-element.65, f32[32,6,384]{2,0,1:T(8,128)S(1)} %get-tuple-element.66, ...), kind=kLoop, calls=%fused_computation.30 | loop fusion | flops 20054016 | bytes 7274496 | tf_op jit(solution)/shard_map/add | solution.py:79
  65.3 2.8 %copy.24 = f32[8,32,6,384]{3,0,2,1:T(8,128)} copy(f32[8,32,6,384]{3,1,2,0:T(8,128)S(1)} %fusion.14) | data formatting | bytes 4718592 | tf_op jit(solution)/shard_map/add | solution.py:79
  69.7 5.9 %copy.25 = f32[8,32,2304]{1,0,2:T(8,128)} copy(f32[8,32,2304]{2,0,1:T(8,128)S(1)} %bitcast.72) | data formatting | bytes 4718592 | tf_op jit(solution)/shard_map/reshape | solution.py:133
  75.6 4.3 %gather_fusion = f32[16,8,32]{2,1,0:T(8,128)S(1)} fusion(f32[8,32,2304]{1,0,2:T(8,128)} %copy.25, s32[1024]{0:T(1024)S(1)} %pad_clamp_fusion), kind=kCustom, calls=%fused_computation | custom fusion | bytes 32832 | tf_op jit(solution)/shard_map/jit(_take)/gather | solution.py:135
  80.3 14.6 %all_to_all.11 = f32[8,1,4096]{2,1,0:T(1,128)S(1)} all-to-all(f32[8,1,4096]{2,1,0:T(1,128)S(1)} %reshape.69), channel_id=1, replica_groups=mesh['rows'=32,'mem'=8] {'mem'}, dimensions={0} | all-to-all | bytes 262144 | tf_op jit(solution)/shard_map/all_to_all | solution.py:36
  99.5 10.2 %all-to-all-start.1 = ((f32[32,1,4160]{2,1,0:T(1,128)}), f32[32,1,4160]{2,1,0:T(1,128)S(1)}, u32[]{:S(2)}, u32[]{:S(2)}) async-start(f32[32,1,4160]{2,1,0:T(1,128)} %broadcast_in_dim.25), calls=%async_computation.1 | async-start | bytes 1081344 | tf_op jit(solution)/shard_map/all_to_all | solution.py:36
  109.8 14.8 %all-to-all-done.1 = f32[32,1,4160]{2,1,0:T(1,128)S(1)} async-done(((f32[32,1,4160]{2,1,0:T(1,128)}), f32[32,1,4160]{2,1,0:T(1,128)S(1)}, u32[]{:S(2)}, u32[]{:S(2)}) %all-to-all-start.1) | async-done | bytes 532512 | tf_op jit(solution)/shard_map/all_to_all | solution.py:36
  126.5 2.6 %while.13 = (s32[]{:T(128)}, f32[64,64]{0,1:T(8,128)S(1)}, f32[64,64]{1,0:T(8,128)S(1)}, s32[]{:T(128)}) while((s32[]{:T(128)}, f32[64,64]{0,1:T(8,128)S(1)}, f32[64,64]{1,0:T(8,128)S(1)}, s32[]{:T(128)}) %tuple.37), condition=%wide.region_4.5_spmd.clone, body=%wide.region_3.4_spmd.clone.sunk | while | flops 9453570 | bytes 213045 | solution.py:109
  129.7 40.7 %all-gather.2.cloned.1.call-done = f32[64,32,2304]{2,0,1:T(8,128)} async-done(((f32[8,32,2304]{2,0,1:T(8,128)}), f32[64,32,2304]{2,0,1:T(8,128)}) %all-gather.2.cloned.1.call-update) | async-done | bytes 18874384 | tf_op jit(solution)/shard_map/all_gather | solution.py:145
  170.4 12.0 %fusion.69 = f32[8,32,2304]{2,0,1:T(8,128)S(1)} fusion(f32[64,32,2304]{2,0,1:T(8,128)} %all-gather.2.cloned.1.call-done, f32[64,64]{0,1:T(8,128)S(1)} %fusion.61, s32[]{:T(128)S(6)} %select_n.14), kind=kOutput, calls=%fused_computation.113 | convolution fusion | flops 452985344 | bytes 21237764 | tf_op jit(solution)/shard_map/jk,jzc->kzc/dot_general | solution.py:142
  182.4 2.1 %copy.31 = f32[8,32,6,384]{3,1,2,0:T(8,128)} copy(f32[8,32,6,384]{3,0,2,1:T(8,128)S(1)} %bitcast.73) | data formatting | bytes 4718592 | tf_op jit(solution)/shard_map/reshape | solution.py:148
  (65 shorter events, 14.8 us)
Async XLA Ops:
  6.5 17.7 %copy-start.1 = (f32[8,32,6,384]{3,1,2,0:T(8,128)S(1)}, f32[8,32,6,384]{3,1,2,0:T(8,128)}, u32[]{:S(2)}) copy-start(f32[8,32,6,384]{3,1,2,0:T(8,128)} %param.7) | copy-start | bytes 7077892
  6.5 163.9 %all-gather.2.cloned.1.call-start = ((), (), s32[]{:S(2)}) async-start(), calls=%async_computation.2 | async-start | bytes 21233664 | tf_op jit(solution)/shard_map/all_gather | solution.py:145
  7.9 12.1 %collective-permute-start = (f32[8,32,1,384]{3,1,2,0:T(8,128)S(1)}, f32[8,32,1,384]{3,1,2,0:T(8,128)S(1)}, u32[]{:S(2)}, u32[]{:S(2)}) collective-permute-start(f32[8,32,1,384]{3,1,2,0:T(8,128)S(1)} %get-tuple-element.60), channel_id=1, source_target_pairs={{0,8},{8,16},{16,24},{24,32},{32,40},{40,48},{48,56},{56,64},{64,7... | collective-permute-start | bytes 1179656 | tf_op jit(solution)/shard_map/ppermute | solution.py:19
  12.3 11.9 %collective-permute-start.1 = (f32[8,32,1,384]{3,1,2,0:T(8,128)S(1)}, f32[8,32,1,384]{3,1,2,0:T(8,128)S(1)}, u32[]{:S(2)}, u32[]{:S(2)}) collective-permute-start(f32[8,32,1,384]{3,1,2,0:T(8,128)S(1)} %get-tuple-element.61), channel_id=1, source_target_pairs={{8,0},{16,8},{24,16},{32,24},{40,32},{48,40},{56,48},{64,56},{72,6... | collective-permute-start | bytes 1179656 | tf_op jit(solution)/shard_map/ppermute | solution.py:21
  28.0 10.4 %collective-permute-start.2 = (f32[8,32,1,384]{3,1,2,0:T(8,128)S(1)}, f32[8,32,1,384]{3,1,2,0:T(8,128)S(1)}, u32[]{:S(2)}, u32[]{:S(2)}) collective-permute-start(f32[8,32,1,384]{3,1,2,0:T(8,128)S(1)} %get-tuple-element.58), channel_id=1, source_target_pairs={{0,8},{8,16},{16,24},{24,32},{32,40},{40,48},{48,56},{56,64},{64,7... | collective-permute-start | bytes 1179656 | tf_op jit(solution)/shard_map/ppermute | solution.py:19
  31.6 12.5 %collective-permute-start.3 = (f32[8,32,1,384]{3,1,2,0:T(8,128)S(1)}, f32[8,32,1,384]{3,1,2,0:T(8,128)S(1)}, u32[]{:S(2)}, u32[]{:S(2)}) collective-permute-start(f32[8,32,1,384]{3,1,2,0:T(8,128)S(1)} %get-tuple-element.59), channel_id=1, source_target_pairs={{8,0},{16,8},{24,16},{32,24},{40,32},{48,40},{56,48},{64,56},{72,6... | collective-permute-start | bytes 1179656 | tf_op jit(solution)/shard_map/ppermute | solution.py:21
  47.9 9.8 %collective-permute-start.4 = (f32[8,32,1,384]{3,1,2,0:T(8,128)S(1)}, f32[8,32,1,384]{3,1,2,0:T(8,128)S(1)}, u32[]{:S(2)}, u32[]{:S(2)}) collective-permute-start(f32[8,32,1,384]{3,1,2,0:T(8,128)S(1)} %get-tuple-element.56), channel_id=1, source_target_pairs={{0,8},{8,16},{16,24},{24,32},{32,40},{40,48},{48,56},{56,64},{64,7... | collective-permute-start | bytes 1179656 | tf_op jit(solution)/shard_map/ppermute | solution.py:19
  51.9 9.6 %collective-permute-start.5 = (f32[8,32,1,384]{3,1,2,0:T(8,128)S(1)}, f32[8,32,1,384]{3,1,2,0:T(8,128)S(1)}, u32[]{:S(2)}, u32[]{:S(2)}) collective-permute-start(f32[8,32,1,384]{3,1,2,0:T(8,128)S(1)} %get-tuple-element.57), channel_id=1, source_target_pairs={{8,0},{16,8},{24,16},{32,24},{40,32},{48,40},{56,48},{64,56},{72,6... | collective-permute-start | bytes 1179656 | tf_op jit(solution)/shard_map/ppermute | solution.py:21
  68.1 0.7 copy-start.4
  68.1 1.7 copy-start
  75.6 21.2 %copy-start.2 = (f32[32,16]{0,1:T(8,128)S(1)}, f32[32,16]{0,1:T(8,128)}, u32[]{:S(2)}) copy-start(f32[32,16]{0,1:T(8,128)} %param.11) | copy-start | bytes 6148
  75.6 21.2 %copy-start.3 = (f32[32,16]{0,1:T(8,128)S(1)}, f32[32,16]{0,1:T(8,128)}, u32[]{:S(2)}) copy-start(f32[32,16]{0,1:T(8,128)} %param.10) | copy-start | bytes 6148
  99.5 25.1 %all-to-all-start.1 = ((f32[32,1,4160]{2,1,0:T(1,128)}), f32[32,1,4160]{2,1,0:T(1,128)S(1)}, u32[]{:S(2)}, u32[]{:S(2)}) async-start(f32[32,1,4160]{2,1,0:T(1,128)} %broadcast_in_dim.25), calls=%async_computation.1 | async-start | bytes 1081344 | tf_op jit(solution)/shard_map/all_to_all | solution.py:36
Sparse Core Ops, SparseCore 0:
  68.2 102.1 all-gather.1
where the time goes:
time: 192 us; the launch traced here: 191 us
  waiting for transfers between devices  84.3 us (44%)
  starting transfers between devices  26.1 us (14%)
  local copies, waits for them, and re-layouts  20.6 us (11%)
  matrix products  16.3 us (8%)
  other arithmetic  14.8 us (8%)
  blocking collectives  14.6 us (8%)
  between operations  14.4 us (8%)
    all_gather x1, waiting for transfers between devices, per_device(): lax.all_gather(state_vectors, 'mem', axis=0, tiled=True)  40.7 us
    ppermute x3, waiting for transfers between devices, padded_2(): lax.ppermute(tail, axis, [(i, (i + 1) % count) for i in range(ends)])  15.1 us
    all_to_all x1, waiting for transfers between devices, from_everyone(): return lax.all_to_all(copies, axis, split_axis=0, concat_axis=0, tiled=True)  14.8 us
    all_to_all x1, blocking collectives, from_everyone(): return lax.all_to_all(copies, axis, split_axis=0, concat_axis=0, tiled=True)  14.6 us
    ppermute x3, waiting for transfers between devices, padded_2(): lax.ppermute(head, axis, [((i + 1) % count, i) for i in range(ends)])  13.7 us
    ppermute x3, starting transfers between devices, padded_2(): lax.ppermute(tail, axis, [(i, (i + 1) % count) for i in range(ends)])  12 us
    dot_general x1, matrix products, per_device(): jnp.einsum('jk,jzc->kzc', own_columns, lax.all_gather(state_vectors, 'mem...  12 us
    add x3, other arithmetic, advance(): return center + change  11.2 us
  transfers between devices with their start and end apart: 8, of which 8 were waited for; matrix products, arithmetic and copies ran while one was open for 11% of the time, Pallas kernels for 0%

commit v1 on v0

--- a/solution.py
+++ b/solution.py
@@ -6,6 +6,28 @@
 STEPS = 3
 NS_ITERS = 4
 DIFFUSION = 0.05
+
+
+def in_order(blocks, dim):
+    blocks = jnp.moveaxis(blocks, 0, dim)
+    shape = blocks.shape
+    return blocks.reshape(*shape[:dim], shape[dim] * shape[dim + 1], *shape[dim + 2 :])
+
+
+def ring_gather(x, axis, dim):
+    devices = lax.axis_size(axis)
+    pairs = [(i, (i + 1) % devices) for i in range(devices)]
+    back = [(b, a) for a, b in pairs]
+    lower, upper = ([], [])
+    for turn in range(devices - 1):
+        if turn % 2 == 0:
+            lower.append(lax.ppermute(lower[-1] if lower else x, axis, pairs))
+        else:
+            upper.append(lax.ppermute(upper[-1] if upper else x, axis, back))
+    blocks = jnp.stack([*lower[::-1], x, *upper])
+    shift = lax.axis_index(axis) - len(lower)
+    blocks = blocks[(jnp.arange(devices) - shift) % devices]
+    return in_order(blocks, dim)
 
 
 def padded_2(cells, sides, width):
@@ -142,7 +164,7 @@
     updated_ensemble = jnp.einsum(
         "jk,jzc->kzc",
         own_columns,
-        lax.all_gather(state_vectors, "mem", axis=0, tiled=True),
+        ring_gather(state_vectors, "mem", 0),
         precision=lax.Precision.HIGHEST,
     )
     return updated_ensemble.reshape(concentration.shape)

time: 192 us -> 262 us (1.36); the launches traced: 191 us -> 257 us
  local copies, waits for them, and re-layouts: 20.6 us -> 73.5 us
  starting transfers between devices: 26.1 us -> 54.2 us
  blocking collectives: 14.6 us -> 0 us
  between operations: 14.4 us -> 1.18 us
  other arithmetic: 14.8 us -> 22.8 us
  waiting for transfers between devices: 84.3 us -> 91.3 us
    ppermute x0 -> x7, waiting for transfers between devices: none -> 54.7 us  [the longest x3 28.9 us: ring_gather(): upper.append(lax.ppermute(upper[-1] if upper else x, axis, back))]
    all_gather x1 -> x0, waiting for transfers between devices: 40.7 us -> none  [per_device(): lax.all_gather(state_vectors, 'mem', axis=0, tiled=True)]
    unnamed x14 -> x39, local copies, waits for them, and re-layouts: 2.17 us -> 23.3 us
    gather x0 -> x1, local copies, waits for them, and re-layouts: none -> 15.3 us  [ring_gather(): blocks = blocks[(jnp.arange(devices) - shift) % devices]]
    all_to_all x1 -> x0, blocking collectives: 14.6 us -> none  [from_everyone(): return lax.all_to_all(copies, axis, split_axis=0, concat_axis=0, tiled=True)]
    ppermute x0 -> x7, starting transfers between devices: none -> 13 us  [the longest x4 7.79 us: ring_gather(): lower.append(lax.ppermute(lower[-1] if lower else x, axis, pairs))]
    ppermute x3, waiting for transfers between devices: 15.1 us -> 2.7 us  [padded_2(): lax.ppermute(tail, axis, [(i, (i + 1) % count) for i in range(ends)])]
    all_to_all x1 -> x2, starting transfers between devices: 10.2 us -> 21.2 us  [from_everyone(): return lax.all_to_all(copies, axis, split_axis=0, concat_axis=0, tiled=True)]
  transfers between devices with their start and end apart: 8 -> 15, of which waited for: 8 -> 11; matrix products, arithmetic and copies ran while one was open for 11% -> 22% of each run, Pallas kernels for 0% -> 0%
where the time goes in v1:
time: 262 us; the launch traced here: 257 us
  waiting for transfers between devices  91.3 us (35%)
  local copies, waits for them, and re-layouts  73.5 us (28%)
  starting transfers between devices  54.2 us (21%)
  other arithmetic  22.8 us (9%)
  matrix products  14.1 us (5%)
    ppermute x3, waiting for transfers between devices, ring_gather(): upper.append(lax.ppermute(upper[-1] if upper else x, axis, back))  28.9 us
    ppermute x4, waiting for transfers between devices, ring_gather(): lower.append(lax.ppermute(lower[-1] if lower else x, axis, pairs))  25.8 us
    unnamed x39, local copies, waits for them, and re-layouts  23.3 us
    all_to_all x2, starting transfers between devices, from_everyone(): return lax.all_to_all(copies, axis, split_axis=0, concat_axis=0, tiled=True)  21.2 us
    all_to_all x2, waiting for transfers between devices, from_everyone(): return lax.all_to_all(copies, axis, split_axis=0, concat_axis=0, tiled=True)  19.9 us
    ppermute x3, starting transfers between devices, padded_2(): lax.ppermute(tail, axis, [(i, (i + 1) % count) for i in range(ends)])  16.1 us
    gather x1, local copies, waits for them, and re-layouts, ring_gather(): blocks = blocks[(jnp.arange(devices) - shift) % devices]  15.3 us
    ppermute x3, waiting for transfers between devices, padded_2(): lax.ppermute(head, axis, [((i + 1) % count, i) for i in range(ends)])  14 us
  transfers between devices with their start and end apart: 15, of which 11 were waited for; matrix products, arithmetic and copies ran while one was open for 22% of the time, Pallas kernels for 0%

profile of v1, /device:TPU:1, one launch (start us, length us, event | category | flops | bytes accessed | tf_op | source)
XLA Modules:
  0.0 257.4 jit_solution(10464091985023362619)
XLA Ops:
  2.6 5.0 %collective-permute-start = (f32[8,32,1,384]{3,1,2,0:T(8,128)S(1)}, f32[8,32,1,384]{3,1,2,0:T(8,128)S(1)}, u32[]{:S(2)}, u32[]{:S(2)}) collective-permute-start(f32[8,32,1,384]{3,1,2,0:T(8,128)S(1)} %get-tuple-element.60), channel_id=1, source_target_pairs={{0,8},{8,16},{16,24},{24,32},{32,40},{40,48},{48,56},{56,64},{64,7... | collective-permute-start | bytes 1179656 | tf_op jit(solution)/shard_map/ppermute | solution.py:41
  9.0 3.7 %collective-permute-done.1 = f32[8,32,1,384]{3,1,2,0:T(8,128)S(1)} collective-permute-done((f32[8,32,1,384]{3,1,2,0:T(8,128)S(1)}, f32[8,32,1,384]{3,1,2,0:T(8,128)S(1)}, u32[]{:S(2)}, u32[]{:S(2)}) %collective-permute-start.1) | collective-permute-done | bytes 393248 | tf_op jit(solution)/shard_map/ppermute | solution.py:43
  13.6 3.7 %fusion.51 = f32[8,32,6,384]{3,1,2,0:T(8,128)S(1)} fusion(f32[8,32,6,384]{3,1,2,0:T(8,128)S(1)} %copy-done.7, f32[8,32,1,384]{3,1,2,0:T(8,128)S(1)} %collective-permute-done.1, f32[8,32,1,384]{3,1,2,0:T(8,128)S(1)} %collective-permute-done, f32[32,6,384]{2,0,1:T(8,128)S(1)} %get-tuple-element.65, f32[32,6,384]{2,0,1:T(8,128)S(1)} %get-tuple-element.66, ...), kind=kLoop, calls=%fused_computation.72 | loop fusion | flops 20054016 | bytes 7274496 | tf_op jit(solution)/shard_map/add | solution.py:101
  18.7 5.9 %collective-permute-start.2 = (f32[8,32,1,384]{3,1,2,0:T(8,128)S(1)}, f32[8,32,1,384]{3,1,2,0:T(8,128)S(1)}, u32[]{:S(2)}, u32[]{:S(2)}) collective-permute-start(f32[8,32,1,384]{3,1,2,0:T(8,128)S(1)} %get-tuple-element.58), channel_id=1, source_target_pairs={{0,8},{8,16},{16,24},{24,32},{32,40},{40,48},{48,56},{56,64},{64,7... | collective-permute-start | bytes 1179656 | tf_op jit(solution)/shard_map/ppermute | solution.py:41
  24.6 5.3 %collective-permute-done.3 = f32[8,32,1,384]{3,1,2,0:T(8,128)S(1)} collective-permute-done((f32[8,32,1,384]{3,1,2,0:T(8,128)S(1)}, f32[8,32,1,384]{3,1,2,0:T(8,128)S(1)}, u32[]{:S(2)}, u32[]{:S(2)}) %collective-permute-start.3) | collective-permute-done | bytes 393248 | tf_op jit(solution)/shard_map/ppermute | solution.py:43
  30.9 3.7 %fusion.34 = f32[8,32,6,384]{3,1,2,0:T(8,128)S(1)} fusion(f32[8,32,6,384]{3,1,2,0:T(8,128)S(1)} %fusion.51, f32[8,32,1,384]{3,1,2,0:T(8,128)S(1)} %collective-permute-done.3, f32[8,32,1,384]{3,1,2,0:T(8,128)S(1)} %collective-permute-done.2, f32[32,6,384]{2,0,1:T(8,128)S(1)} %get-tuple-element.65, f32[32,6,384]{2,0,1:T(8,128)S(1)} %get-tuple-element.66, ...), kind=kLoop, calls=%fused_computation.53 | loop fusion | flops 20054016 | bytes 7274496 | tf_op jit(solution)/shard_map/add | solution.py:101
  36.0 5.2 %collective-permute-start.4 = (f32[8,32,1,384]{3,1,2,0:T(8,128)S(1)}, f32[8,32,1,384]{3,1,2,0:T(8,128)S(1)}, u32[]{:S(2)}, u32[]{:S(2)}) collective-permute-start(f32[8,32,1,384]{3,1,2,0:T(8,128)S(1)} %get-tuple-element.56), channel_id=1, source_target_pairs={{0,8},{8,16},{16,24},{24,32},{32,40},{40,48},{48,56},{56,64},{64,7... | collective-permute-start | bytes 1179656 | tf_op jit(solution)/shard_map/ppermute | solution.py:41
  41.2 4.9 %collective-permute-done.5 = f32[8,32,1,384]{3,1,2,0:T(8,128)S(1)} collective-permute-done((f32[8,32,1,384]{3,1,2,0:T(8,128)S(1)}, f32[8,32,1,384]{3,1,2,0:T(8,128)S(1)}, u32[]{:S(2)}, u32[]{:S(2)}) %collective-permute-start.5) | collective-permute-done | bytes 393248 | tf_op jit(solution)/shard_map/ppermute | solution.py:43
  47.1 3.7 %fusion.91 = f32[8,6,4,8,384]{4,3,2,1,0:T(8,128)S(1)} fusion(f32[8,32,6,384]{3,1,2,0:T(8,128)S(1)} %fusion.34, f32[32,6,384]{2,0,1:T(8,128)S(1)} %get-tuple-element.65, f32[32,6,384]{2,0,1:T(8,128)S(1)} %get-tuple-element.66, f32[32,6,384]{2,0,1:T(8,128)S(1)} %get-tuple-element.64, f32[32,6,384]{2,0,1:T(8,128)S(1)} %get-tuple-element.67, ...), kind=kLoop, calls=%fused_computation.147 | loop fusion | flops 20054016 | bytes 7274496
  52.4 5.2 %collective-permute-start.6 = (f32[8,32,2304]{2,1,0:T(8,128)S(1)}, f32[8,32,2304]{2,1,0:T(8,128)}, u32[]{:S(2)}, u32[]{:S(2)}) collective-permute-start(f32[8,32,2304]{2,1,0:T(8,128)S(1)} %bitcast.97), channel_id=1, source_target_pairs={{0,1},{1,2},{2,3},{3,4},{4,5},{5,6},{6,7},{7,0},{8,9},{9,10},{10,1... | collective-permute-start | bytes 7077896 | tf_op jit(solution)/shard_map/ppermute | solution.py:24
  57.6 25.8 %collective-permute-done.6 = f32[8,32,2304]{2,1,0:T(8,128)} collective-permute-done((f32[8,32,2304]{2,1,0:T(8,128)S(1)}, f32[8,32,2304]{2,1,0:T(8,128)}, u32[]{:S(2)}, u32[]{:S(2)}) %collective-permute-start.6) | collective-permute-done | bytes 2359328 | tf_op jit(solution)/shard_map/ppermute | solution.py:24
  86.0 6.8 %copy.29 = f32[8,32,2304]{1,0,2:T(8,128)} copy(f32[8,32,2304]{2,1,0:T(8,128)} %bitcast.98) | data formatting | bytes 4718592 | tf_op jit(solution)/shard_map/reshape | solution.py:155
  92.8 4.3 %gather_fusion = f32[16,8,32]{2,1,0:T(8,128)S(1)} fusion(f32[8,32,2304]{1,0,2:T(8,128)} %copy.29, s32[1024]{0:T(1024)S(1)} %pad_clamp_fusion.1), kind=kCustom, calls=%fused_computation | custom fusion | bytes 32832 | tf_op jit(solution)/shard_map/jit(_take)/gather | solution.py:157
  98.2 4.1 %all-to-all-start = ((f32[8,1,4096]{2,1,0:T(1,128)}), f32[8,1,4096]{2,1,0:T(1,128)S(1)}, u32[]{:S(2)}, u32[]{:S(2)}) async-start(f32[8,1,4096]{2,1,0:T(1,128)} %reshape.128), calls=%async_computation | async-start | bytes 262144 | tf_op jit(solution)/shard_map/all_to_all | solution.py:58
  103.0 13.3 %all-to-all-done = f32[8,1,4096]{2,1,0:T(1,128)S(1)} async-done(((f32[8,1,4096]{2,1,0:T(1,128)}), f32[8,1,4096]{2,1,0:T(1,128)S(1)}, u32[]{:S(2)}, u32[]{:S(2)}) %all-to-all-start) | async-done | bytes 131104 | tf_op jit(solution)/shard_map/all_to_all | solution.py:58
  125.0 17.1 %all-to-all-start.1 = ((f32[32,1,4160]{2,1,0:T(1,128)}), f32[32,1,4160]{2,1,0:T(1,128)}, u32[]{:S(2)}, u32[]{:S(2)}) async-start(f32[32,1,4160]{2,1,0:T(1,128)} %broadcast_in_dim.26), calls=%async_computation.1 | async-start | bytes 1081344 | tf_op jit(solution)/shard_map/all_to_all | solution.py:58
  142.1 5.0 %fusion.17 = f32[8,32,6,384]{3,1,2,0:T(8,128)S(1)} fusion(f32[8,32,6,384]{3,1,2,0:T(8,128)S(1)} %fusion.34, f32[8,32,1,384]{3,1,2,0:T(8,128)} %copy-done.8, f32[8,32,1,384]{3,1,2,0:T(8,128)} %copy-done.9, f32[32,6,384]{2,0,1:T(8,128)} %copy-done.4, f32[32,6,384]{2,0,1:T(8,128)} %copy-done.5, f32[32,6,384]{2,0,1:T(8,128)S(1)} %copy-done.3, ...), kind=kLoop, calls=%fused_computation.34 | loop fusion | flops 20054016 | bytes 7274496 | tf_op jit(solution)/shard_map/add | solution.py:101
  150.2 6.5 %all-to-all-done.1 = f32[32,1,4160]{2,1,0:T(1,128)} async-done(((f32[32,1,4160]{2,1,0:T(1,128)}), f32[32,1,4160]{2,1,0:T(1,128)}, u32[]{:S(2)}, u32[]{:S(2)}) %all-to-all-start.1) | async-done | bytes 532512 | tf_op jit(solution)/shard_map/all_to_all | solution.py:58
  165.9 22.8 %collective-permute-done.11 = f32[8,32,2304]{2,1,0:T(8,128)S(1)} collective-permute-done((f32[8,32,2304]{2,1,0:T(8,128)}, f32[8,32,2304]{2,1,0:T(8,128)S(1)}, u32[]{:S(2)}, u32[]{:S(2)}) %collective-permute-start.11) | collective-permute-done | bytes 2359328 | tf_op jit(solution)/shard_map/ppermute | solution.py:26
  200.9 3.5 %bitcast_dynamic-update-slice_fusion.3 = f32[8,8,32,2304]{3,2,1,0:T(8,128)} fusion(f32[8,8,32,2304]{3,2,1,0:T(8,128)} %bitcast_dynamic-update-slice_fusion.4, f32[8,32,2304]{2,1,0:T(8,128)} %collective-permute-done.6), kind=kLoop, calls=%fused_computation.82 | loop fusion | bytes 4718592
  210.8 6.1 %collective-permute-done.12 = f32[8,32,2304]{2,1,0:T(8,128)S(1)} collective-permute-done((f32[8,32,2304]{2,1,0:T(8,128)S(1)}, f32[8,32,2304]{2,1,0:T(8,128)S(1)}, u32[]{:S(2)}, u32[]{:S(2)}) %collective-permute-start.12) | collective-permute-done | bytes 2359328 | tf_op jit(solution)/shard_map/ppermute | solution.py:26
  218.5 15.3 %gather_fusion.1 = f32[8,8,32,2304]{3,2,1,0:T(8,128)} fusion(f32[8,8,32,2304]{3,2,1,0:T(8,128)} %bitcast_dynamic-update-slice_fusion, s32[1024]{0:T(1024)S(1)} %pad_clamp_fusion), kind=kCustom, calls=%fused_computation.1 | custom fusion | bytes 37748768 | tf_op jit(solution)/shard_map/gather | solution.py:29
  233.8 12.3 %copy.36 = f32[64,32,2304]{2,0,1:T(8,128)S(1)} copy(f32[64,32,2304]{2,1,0:T(8,128)} %bitcast.95) | data formatting | bytes 37748736 | tf_op jit(solution)/shard_map/reshape | solution.py:14
  246.2 9.1 %fusion.3 = f32[8,32,6,384]{3,0,2,1:T(8,128)S(1)} fusion(f32[32,8,6,8,384]{4,3,2,1,0:T(8,128)S(1)} %bitcast.96, f32[64,64]{0,1:T(8,128)S(1)} %fusion.64, s32[]{:T(128)S(6)} %select_n.38), kind=kOutput, calls=%fused_computation.7 | convolution fusion | flops 452985344 | bytes 21237764 | tf_op jit(solution)/shard_map/jk,jzc->kzc/dot_general | solution.py:164
  (110 shorter events, 60.0 us)
Async XLA Ops:
  0.0 13.6 %copy-start.7 = (f32[8,32,6,384]{3,1,2,0:T(8,128)S(1)}, f32[8,32,6,384]{3,1,2,0:T(8,128)}, u32[]{:S(2)}) copy-start(f32[8,32,6,384]{3,1,2,0:T(8,128)} %param.7) | copy-start | bytes 7077892
  1.3 11.4 %collective-permute-start.1 = (f32[8,32,1,384]{3,1,2,0:T(8,128)S(1)}, f32[8,32,1,384]{3,1,2,0:T(8,128)S(1)}, u32[]{:S(2)}, u32[]{:S(2)}) collective-permute-start(f32[8,32,1,384]{3,1,2,0:T(8,128)S(1)} %get-tuple-element.61), channel_id=1, source_target_pairs={{8,0},{16,8},{24,16},{32,24},{40,32},{48,40},{56,48},{64,56},{72,6... | collective-permute-start | bytes 1179656 | tf_op jit(solution)/shard_map/ppermute | solution.py:43
  2.6 11.0 %collective-permute-start = (f32[8,32,1,384]{3,1,2,0:T(8,128)S(1)}, f32[8,32,1,384]{3,1,2,0:T(8,128)S(1)}, u32[]{:S(2)}, u32[]{:S(2)}) collective-permute-start(f32[8,32,1,384]{3,1,2,0:T(8,128)S(1)} %get-tuple-element.60), channel_id=1, source_target_pairs={{0,8},{8,16},{16,24},{24,32},{32,40},{40,48},{48,56},{56,64},{64,7... | collective-permute-start | bytes 1179656 | tf_op jit(solution)/shard_map/ppermute | solution.py:41
  8.9 38.1 %copy-start.2 = (f32[32,6,384]{2,0,1:T(8,128)}, f32[32,6,384]{2,0,1:T(8,128)S(1)}, u32[]{:S(2)}) copy-start(f32[32,6,384]{2,0,1:T(8,128)S(1)} %get-tuple-element.64) | copy-start | bytes 884740
  8.9 38.1 %copy-start.4 = (f32[32,6,384]{2,0,1:T(8,128)}, f32[32,6,384]{2,0,1:T(8,128)S(1)}, u32[]{:S(2)}) copy-start(f32[32,6,384]{2,0,1:T(8,128)S(1)} %get-tuple-element.65) | copy-start | bytes 884740
  8.9 38.1 %copy-start.5 = (f32[32,6,384]{2,0,1:T(8,128)}, f32[32,6,384]{2,0,1:T(8,128)S(1)}, u32[]{:S(2)}) copy-start(f32[32,6,384]{2,0,1:T(8,128)S(1)} %get-tuple-element.66) | copy-start | bytes 884740
  9.0 38.1 %copy-start.6 = (f32[32,6,384]{2,0,1:T(8,128)}, f32[32,6,384]{2,0,1:T(8,128)S(1)}, u32[]{:S(2)}) copy-start(f32[32,6,384]{2,0,1:T(8,128)S(1)} %get-tuple-element.67) | copy-start | bytes 884740
  17.4 12.5 %collective-permute-start.3 = (f32[8,32,1,384]{3,1,2,0:T(8,128)S(1)}, f32[8,32,1,384]{3,1,2,0:T(8,128)S(1)}, u32[]{:S(2)}, u32[]{:S(2)}) collective-permute-start(f32[8,32,1,384]{3,1,2,0:T(8,128)S(1)} %get-tuple-element.59), channel_id=1, source_target_pairs={{8,0},{16,8},{24,16},{32,24},{40,32},{48,40},{56,48},{64,56},{72,6... | collective-permute-start | bytes 1179656 | tf_op jit(solution)/shard_map/ppermute | solution.py:43
  18.7 12.1 %collective-permute-start.2 = (f32[8,32,1,384]{3,1,2,0:T(8,128)S(1)}, f32[8,32,1,384]{3,1,2,0:T(8,128)S(1)}, u32[]{:S(2)}, u32[]{:S(2)}) collective-permute-start(f32[8,32,1,384]{3,1,2,0:T(8,128)S(1)} %get-tuple-element.58), channel_id=1, source_target_pairs={{0,8},{8,16},{16,24},{24,32},{32,40},{40,48},{48,56},{56,64},{64,7... | collective-permute-start | bytes 1179656 | tf_op jit(solution)/shard_map/ppermute | solution.py:41
  34.7 11.5 %collective-permute-start.5 = (f32[8,32,1,384]{3,1,2,0:T(8,128)S(1)}, f32[8,32,1,384]{3,1,2,0:T(8,128)S(1)}, u32[]{:S(2)}, u32[]{:S(2)}) collective-permute-start(f32[8,32,1,384]{3,1,2,0:T(8,128)S(1)} %get-tuple-element.57), channel_id=1, source_target_pairs={{8,0},{16,8},{24,16},{32,24},{40,32},{48,40},{56,48},{64,56},{72,6... | collective-permute-start | bytes 1179656 | tf_op jit(solution)/shard_map/ppermute | solution.py:43
  36.0 11.1 %collective-permute-start.4 = (f32[8,32,1,384]{3,1,2,0:T(8,128)S(1)}, f32[8,32,1,384]{3,1,2,0:T(8,128)S(1)}, u32[]{:S(2)}, u32[]{:S(2)}) collective-permute-start(f32[8,32,1,384]{3,1,2,0:T(8,128)S(1)} %get-tuple-element.56), channel_id=1, source_target_pairs={{0,8},{8,16},{16,24},{24,32},{32,40},{40,48},{48,56},{56,64},{64,7... | collective-permute-start | bytes 1179656 | tf_op jit(solution)/shard_map/ppermute | solution.py:41
  50.8 35.2 %copy-start.13 = (s32[16]{0:T(128)S(1)}, s32[16]{0:T(128)}, u32[]{:S(2)}) copy-start(s32[16]{0:T(128)} %param.9) | copy-start | bytes 196
  52.4 31.0 %collective-permute-start.6 = (f32[8,32,2304]{2,1,0:T(8,128)S(1)}, f32[8,32,2304]{2,1,0:T(8,128)}, u32[]{:S(2)}, u32[]{:S(2)}) collective-permute-start(f32[8,32,2304]{2,1,0:T(8,128)S(1)} %bitcast.97), channel_id=1, source_target_pairs={{0,1},{1,2},{2,3},{3,4},{4,5},{5,6},{6,7},{7,0},{8,9},{9,10},{10,1... | collective-permute-start | bytes 7077896 | tf_op jit(solution)/shard_map/ppermute | solution.py:24
  83.4 36.8 %collective-permute-start.7 = (f32[8,32,2304]{2,1,0:T(8,128)}, f32[8,32,2304]{2,1,0:T(8,128)}, u32[]{:S(2)}, u32[]{:S(2)}) collective-permute-start(f32[8,32,2304]{2,1,0:T(8,128)} %collective-permute-done.6), channel_id=1, source_target_pairs={{0,1},{1,2},{2,3},{3,4},{4,5},{5,6},{6,7},{7,0},{8,9},{9,10},{10,1... | collective-permute-start | bytes 7077896 | tf_op jit(solution)/shard_map/ppermute | solution.py:24
  92.8 26.8 %copy-start.11 = (f32[32,16]{0,1:T(8,128)S(1)}, f32[32,16]{0,1:T(8,128)}, u32[]{:S(2)}) copy-start(f32[32,16]{0,1:T(8,128)} %param.11) | copy-start | bytes 6148
  92.8 26.8 %copy-start.12 = (f32[32,16]{0,1:T(8,128)S(1)}, f32[32,16]{0,1:T(8,128)}, u32[]{:S(2)}) copy-start(f32[32,16]{0,1:T(8,128)} %param.10) | copy-start | bytes 6148
  98.2 18.1 %all-to-all-start = ((f32[8,1,4096]{2,1,0:T(1,128)}), f32[8,1,4096]{2,1,0:T(1,128)S(1)}, u32[]{:S(2)}, u32[]{:S(2)}) async-start(f32[8,1,4096]{2,1,0:T(1,128)} %reshape.128), calls=%async_computation | async-start | bytes 262144 | tf_op jit(solution)/shard_map/all_to_all | solution.py:58
  103.0 56.7 %collective-permute-start.10 = (f32[8,32,2304]{2,1,0:T(8,128)}, f32[8,32,2304]{2,1,0:T(8,128)}, u32[]{:S(2)}, u32[]{:S(2)}) collective-permute-start(f32[8,32,2304]{2,1,0:T(8,128)} %bitcast.99), channel_id=1, source_target_pairs={{1,0},{2,1},{3,2},{4,3},{5,4},{6,5},{7,6},{0,7},{9,8},{10,9},{11,1... | collective-permute-start | bytes 7077896 | tf_op jit(solution)/shard_map/ppermute | solution.py:26
  120.2 42.4 %collective-permute-start.8 = (f32[8,32,2304]{2,1,0:T(8,128)}, f32[8,32,2304]{2,1,0:T(8,128)}, u32[]{:S(2)}, u32[]{:S(2)}) collective-permute-start(f32[8,32,2304]{2,1,0:T(8,128)} %collective-permute-done.7), channel_id=1, source_target_pairs={{0,1},{1,2},{2,3},{3,4},{4,5},{5,6},{6,7},{7,0},{8,9},{9,10},{10,1... | collective-permute-start | bytes 7077896 | tf_op jit(solution)/shard_map/ppermute | solution.py:24
  121.7 20.3 %copy-start.3 = (f32[32,6,384]{2,0,1:T(8,128)S(1)}, f32[32,6,384]{2,0,1:T(8,128)}, u32[]{:S(2)}) copy-start(f32[32,6,384]{2,0,1:T(8,128)} %copy-done.2) | copy-start | bytes 884740
  125.0 31.8 %all-to-all-start.1 = ((f32[32,1,4160]{2,1,0:T(1,128)}), f32[32,1,4160]{2,1,0:T(1,128)}, u32[]{:S(2)}, u32[]{:S(2)}) async-start(f32[32,1,4160]{2,1,0:T(1,128)} %broadcast_in_dim.26), calls=%async_computation.1 | async-start | bytes 1081344 | tf_op jit(solution)/shard_map/all_to_all | solution.py:58
  159.7 29.0 %collective-permute-start.11 = (f32[8,32,2304]{2,1,0:T(8,128)}, f32[8,32,2304]{2,1,0:T(8,128)S(1)}, u32[]{:S(2)}, u32[]{:S(2)}) collective-permute-start(f32[8,32,2304]{2,1,0:T(8,128)} %collective-permute-done.10), channel_id=1, source_target_pairs={{1,0},{2,1},{3,2},{4,3},{5,4},{6,5},{7,6},{0,7},{9,8},{10,9},{11,1... | collective-permute-start | bytes 7077896 | tf_op jit(solution)/shard_map/ppermute | solution.py:26
  162.6 28.4 %collective-permute-start.9 = (f32[8,32,2304]{2,1,0:T(8,128)}, f32[8,32,2304]{2,1,0:T(8,128)}, u32[]{:S(2)}, u32[]{:S(2)}) collective-permute-start(f32[8,32,2304]{2,1,0:T(8,128)} %collective-permute-done.8), channel_id=1, source_target_pairs={{0,1},{1,2},{2,3},{3,4},{4,5},{5,6},{6,7},{7,0},{8,9},{9,10},{10,1... | collective-permute-start | bytes 7077896 | tf_op jit(solution)/shard_map/ppermute | solution.py:24
  188.7 28.3 %collective-permute-start.12 = (f32[8,32,2304]{2,1,0:T(8,128)S(1)}, f32[8,32,2304]{2,1,0:T(8,128)S(1)}, u32[]{:S(2)}, u32[]{:S(2)}) collective-permute-start(f32[8,32,2304]{2,1,0:T(8,128)S(1)} %collective-permute-done.11), channel_id=1, source_target_pairs={{1,0},{2,1},{3,2},{4,3},{5,4},{6,5},{7,6},{0,7},{9,8},{10,9},{11,1... | collective-permute-start | bytes 7077896 | tf_op jit(solution)/shard_map/ppermute | solution.py:26
  (5 other events, 22.9 us)
